TPU v7x, 32 devices: a whole 2x2x4 slice. The times are simulated.
32 devices in a mesh: slides: 2 (over y), seq: 16 (over z, x, core), mp: 1.
Axes of the slice: x: 2, y: 2, z: 4, core: 2. Of those that a mesh axis runs over, the one named last changes fastest.
Arguments:
- tokens: bfloat16 [32768, 768], P(('slides', 'seq', 'mp')), parts along dimension 0, may hold values from -6 to 6
- attn_gain: float32 [768], replicated, may hold values from 0.25 to 1.75
- query_first: bfloat16 [768, 768], P(None, 'mp'), may hold values from -4 to 4
- key_first: bfloat16 [768, 768], P(None, 'mp'), may hold values from -4 to 4
- segment_value: bfloat16 [768, 768], P(None, 'mp'), may hold values from -0.21875 to 0.21875
- output_first: bfloat16 [768, 768], P('mp'), may hold values from -0.875 to 0.875
- mlp_gain: float32 [768], replicated, may hold values from 0.25 to 1.75
- up_weight: bfloat16 [768, 3072], P(None, 'mp'), may hold values from -0.21875 to 0.21875
- down_weight: bfloat16 [3072, 768], P('mp'), may hold values from -0.109375 to 0.109375
- second_gain: float32 [768], replicated, may hold values from 0.25 to 1.75
- query_second: bfloat16 [768, 768], P(None, 'mp'), may hold values from -4 to 4
- key_second: bfloat16 [768, 768], P(None, 'mp'), may hold values from -4 to 4
- value_second: bfloat16 [768, 768], P(None, 'mp'), may hold values from -0.21875 to 0.21875
- output_second: bfloat16 [768, 768], P('mp'), may hold values from -0.875 to 0.875
- segment_offset: int32 [16], P('mp'), may hold values from 0 to 63
- global_offset: int32 [16], P('mp'), may hold values from 0 to 63
Outputs:
- encoded: bfloat16 [32768, 768], P(('slides', 'seq', 'mp')), parts along dimension 0
There are 2 independent parts, one for each index of `slides`. A program takes and returns all parts, laid end to end along the dimension named above; an argument that names none is the same for every part. Nothing has to cross between parts.
All inputs are finite; a program needn't handle non-finite values.
Results may differ from a plain program's by a relative error of at most 0.03.
The roundings to bfloat16 on the way count: a program that leaves them out, or rounds other values in their place, can miss the bound.
Values may be sent and summed in bfloat16 or wider, within the bound.
A program may use at most 128 MiB of HBM per device.

v0:
```python
import jax
import jax.numpy as jnp
from jax import lax
from jax.sharding import PartitionSpec as P

KEYS = 256
SEG_MAX = 16


def swapped(x, axis, apart):
    return lax.ppermute(x, axis, [(i, i ^ 1 << apart) for i in range(lax.axis_size(axis))])


def norm_rows(values, gain):
    center = values - jnp.mean(values, axis=-1, keepdims=True)
    spread = jnp.mean(center * center, axis=-1, keepdims=True)
    return (center * lax.rsqrt(spread + 1e-05) * gain).astype(jnp.bfloat16)


def pick_keys(hidden, offsets, stride, key_weight, value_weight):
    token_count, width = hidden.shape
    head_count = offsets.shape[0]
    head_size = key_weight.shape[1] // head_count
    grouped_rows = hidden.reshape(token_count // stride, stride, width)
    dilation_selector = (
        lax.broadcasted_iota(jnp.int32, (stride, head_count), 0) == offsets[None, :]
    ).astype(jnp.bfloat16)
    chosen = jnp.einsum(
        "nof,oj->njf", grouped_rows, dilation_selector, preferred_element_type=jnp.float32
    ).astype(jnp.bfloat16)
    key_heads = jnp.einsum(
        "xkr,rkf->xkf",
        chosen,
        key_weight.reshape(width, head_count, head_size),
        preferred_element_type=jnp.float32,
    ).astype(jnp.bfloat16)
    value_heads = jnp.einsum(
        "xkr,rkf->xkf",
        chosen,
        value_weight.reshape(width, head_count, head_size),
        preferred_element_type=jnp.float32,
    ).astype(jnp.bfloat16)
    picked = token_count // stride
    return jnp.stack(
        [
            key_heads.reshape(picked, head_count * head_size),
            value_heads.reshape(picked, head_count * head_size),
        ]
    )


def attend_local(query, keyval, head_count):
    token_count, width = query.shape
    head_size = width // head_count
    query_heads = query.reshape(token_count, head_count, head_size)
    key_heads = keyval[0].reshape(-1, head_count, head_size)
    value_heads = keyval[1].reshape(-1, head_count, head_size)
    scores = jnp.einsum(
        "thd,khd->htk", query_heads, key_heads, preferred_element_type=jnp.float32
    ) * head_size ** (-0.5)
    highest = jnp.max(scores, axis=-1, keepdims=True)
    weights = jnp.exp(scores - highest)
    weights = (weights / jnp.sum(weights, axis=-1, keepdims=True)).astype(jnp.bfloat16)
    mixed = jnp.einsum(
        "htk,khd->thd", weights, value_heads, preferred_element_type=jnp.float32
    ).astype(jnp.bfloat16)
    return mixed.reshape(token_count, width)


def merge_branch_pair(mine, other, level, token_position):
    lower = token_position >> level & 1 == 0
    return jnp.where(
        lower, jnp.concatenate((mine, other), axis=1), jnp.concatenate((other, mine), axis=1)
    )


def spread_segment(keyval, seg_span, token_position):
    for level in range(seg_span.bit_length() - 1):
        partner = swapped(keyval, "seq", level)
        keyval = merge_branch_pair(keyval, partner, level, token_position)
    return keyval


def spread_global(keyval_two):
    keyval_two = lax.all_gather(keyval_two, "seq", axis=1, tiled=True)
    return keyval_two


def combine(partial_value, residual_full, need_full):
    row_count = residual_full.shape[0] // lax.axis_size("mp")
    row_start = lax.axis_index("mp") * row_count
    share = lax.psum_scatter(partial_value, "mp", scatter_dimension=0, tiled=True)
    own_rows = lax.dynamic_slice_in_dim(residual_full, row_start, row_count, 0)
    own_rows = (own_rows.astype(jnp.float32) + share).astype(jnp.bfloat16)
    full_rows = lax.all_gather(own_rows, "mp", axis=0, tiled=True) if need_full else own_rows
    return (own_rows, full_rows)


def body(
    tokens,
    attn_gain,
    query_first,
    key_first,
    segment_value,
    output_first,
    mlp_gain,
    up_weight,
    down_weight,
    second_gain,
    query_second,
    key_second,
    value_second,
    output_second,
    segment_offset,
    global_offset,
):
    seq_count = lax.axis_size("seq")
    token_position = lax.axis_index("seq")
    seg_span = min(SEG_MAX, seq_count)
    head_count = segment_offset.shape[0]
    full_rows = lax.all_gather(tokens, "mp", axis=0, tiled=True)
    token_count = full_rows.shape[0]
    hidden = norm_rows(full_rows.astype(jnp.float32), attn_gain)
    query = jnp.dot(hidden, query_first, preferred_element_type=jnp.float32).astype(jnp.bfloat16)
    seg_stride = token_count // (KEYS // seg_span)
    keyval = pick_keys(hidden, segment_offset, seg_stride, key_first, segment_value)
    keyval = spread_segment(keyval, seg_span, token_position)
    mixed = attend_local(query, keyval, head_count)
    partial_value = jnp.dot(mixed, output_first, preferred_element_type=jnp.float32)
    own_rows, first_rows = combine(partial_value, full_rows, True)
    normed = norm_rows(first_rows.astype(jnp.float32), mlp_gain)
    inner = jax.nn.gelu(
        jnp.dot(normed, up_weight, preferred_element_type=jnp.float32), approximate=True
    ).astype(jnp.bfloat16)
    partial_value = jnp.dot(inner, down_weight, preferred_element_type=jnp.float32)
    own_rows, second_rows = combine(partial_value, first_rows, True)
    hidden_two = norm_rows(second_rows.astype(jnp.float32), second_gain)
    query_two = jnp.dot(hidden_two, query_second, preferred_element_type=jnp.float32).astype(
        jnp.bfloat16
    )
    glob_stride = token_count // (KEYS // seq_count)
    keyval_two = pick_keys(hidden_two, global_offset, glob_stride, key_second, value_second)
    keyval_two = spread_global(keyval_two)
    mixed_two = attend_local(query_two, keyval_two, head_count)
    partial_value = jnp.dot(mixed_two, output_second, preferred_element_type=jnp.float32)
    own_rows, unused_rows = combine(partial_value, second_rows, False)
    return own_rows


def solution(mesh):
    placed = (
        P(("slides", "seq", "mp"), None),
        P(),
        P(None, "mp"),
        P(None, "mp"),
        P(None, "mp"),
        P("mp", None),
        P(),
        P(None, "mp"),
        P("mp", None),
        P(),
        P(None, "mp"),
        P(None, "mp"),
        P(None, "mp"),
        P("mp", None),
        P("mp"),
        P("mp"),
    )
    return jax.shard_map(
        body,
        mesh=mesh,
        in_specs=placed,
        out_specs=P(("slides", "seq", "mp"), None),
        check_vma=False,
    )
```

profile of v0, /device:TPU:0, one launch (start us, length us, event | category | flops | bytes accessed | tf_op | source)
XLA Modules:
  0.0 132.9 jit_solution(15052510869012871012)
XLA Ops:
  0.0 2.5 %copy.27 = bf16[768,768]{0,1:T(8,128)(2,1)} copy(bf16[768,768]{1,0:T(8,128)(2,1)} %param.19) | data formatting | bytes 2359296 | tf_op args[3]
  4.0 1.1 copy-done.3
  6.1 2.4 %copy.30 = bf16[768,768]{0,1:T(8,128)(2,1)} copy(bf16[768,768]{1,0:T(8,128)(2,1)} %param.20) | data formatting | bytes 2359296 | tf_op args[4]
  8.5 1.7 %fusion.63 = bf16[16,16,48]{2,0,1:T(8,128)(2,1)S(1)} fusion(bf16[768,16,48]{0,2,1:T(8,128)(2,1)} %bitcast.67, bf16[16,16,768]{2,1,0:T(8,128)(2,1)S(1)} %fusion.60), kind=kOutput, calls=%fused_computation.70 | convolution fusion | flops 18886656 | bytes 1597440 | tf_op jit(solution)/shard_map/xkr,rkf->xkf/dot_general | solution.py:37
  11.8 2.9 %collective-permute-start.1 = (bf16[2,32,768]{2,1,0:T(8,128)(2,1)S(1)}, bf16[2,32,768]{2,1,0:T(8,128)(2,1)S(1)}, u32[]{:S(2)}, u32[]{:S(2)}) collective-permute-start(bf16[2,32,768]{2,1,0:T(8,128)(2,1)S(1)} %maximum_select_fusion.3), channel_id=1, source_target_pairs={{0,2},{1,3},{2,0},{3,1},{4,6},{5,7},{6,4},{7,5},{8,10},{9,11},{10,... | collective-permute-start | bytes 294920 | tf_op jit(solution)/shard_map/ppermute | solution.py:11
  14.7 3.1 %collective-permute-done.1 = bf16[2,32,768]{2,1,0:T(8,128)(2,1)S(1)} collective-permute-done((bf16[2,32,768]{2,1,0:T(8,128)(2,1)S(1)}, bf16[2,32,768]{2,1,0:T(8,128)(2,1)S(1)}, u32[]{:S(2)}, u32[]{:S(2)}) %collective-permute-start.1) | collective-permute-done | bytes 98336 | tf_op jit(solution)/shard_map/ppermute | solution.py:11
  17.9 1.9 %collective-permute-start.2 = (bf16[2,64,768]{2,1,0:T(8,128)(2,1)S(1)}, bf16[2,64,768]{2,1,0:T(8,128)(2,1)S(1)}, u32[]{:S(2)}, u32[]{:S(2)}) collective-permute-start(bf16[2,64,768]{2,1,0:T(8,128)(2,1)S(1)} %maximum_select_fusion.2), channel_id=1, source_target_pairs={{0,4},{1,5},{2,6},{3,7},{4,0},{5,1},{6,2},{7,3},{8,12},{9,13},{10,... | collective-permute-start | bytes 589832 | tf_op jit(solution)/shard_map/ppermute | solution.py:11
  19.8 4.6 %collective-permute-done.2 = bf16[2,64,768]{2,1,0:T(8,128)(2,1)S(1)} collective-permute-done((bf16[2,64,768]{2,1,0:T(8,128)(2,1)S(1)}, bf16[2,64,768]{2,1,0:T(8,128)(2,1)S(1)}, u32[]{:S(2)}, u32[]{:S(2)}) %collective-permute-start.2) | collective-permute-done | bytes 196640 | tf_op jit(solution)/shard_map/ppermute | solution.py:11
  24.4 2.6 %collective-permute-start.3 = (bf16[2,128,768]{2,1,0:T(8,128)(2,1)S(1)}, bf16[2,128,768]{2,1,0:T(8,128)(2,1)S(1)}, u32[]{:S(2)}, u32[]{:S(2)}) collective-permute-start(bf16[2,128,768]{2,1,0:T(8,128)(2,1)S(1)} %maximum_select_fusion.1), channel_id=1, source_target_pairs={{0,8},{1,9},{2,10},{3,11},{4,12},{5,13},{6,14},{7,15},{8,0},{9,1},... | collective-permute-start | bytes 1179656 | tf_op jit(solution)/shard_map/ppermute | solution.py:11
  27.0 2.4 %copy.39 = bf16[768,768]{0,1:T(8,128)(2,1)} copy(bf16[768,768]{1,0:T(8,128)(2,1)} %param.28) | data formatting | bytes 2359296 | tf_op args[12]
  29.4 2.4 %copy.36 = bf16[768,768]{0,1:T(8,128)(2,1)} copy(bf16[768,768]{1,0:T(8,128)(2,1)} %param.27) | data formatting | bytes 2359296 | tf_op args[11]
  31.8 4.3 %convolution_convert_fusion.1 = bf16[1024,768]{0,1:T(8,128)(2,1)} fusion(bf16[1024,768]{1,0:T(8,128)(2,1)} %copy-done.3, bf16[768,768]{1,0:T(8,128)(2,1)} %param.18), kind=kOutput, calls=%fused_computation.57 | convolution fusion | flops 1208745984 | bytes 4325376 | tf_op jit(solution)/shard_map/dot_general | solution.py:124
  36.1 7.4 %collective-permute-done.3 = bf16[2,128,768]{2,1,0:T(8,128)(2,1)S(1)} collective-permute-done((bf16[2,128,768]{2,1,0:T(8,128)(2,1)S(1)}, bf16[2,128,768]{2,1,0:T(8,128)(2,1)S(1)}, u32[]{:S(2)}, u32[]{:S(2)}) %collective-permute-start.3) | collective-permute-done | bytes 393248 | tf_op jit(solution)/shard_map/ppermute | solution.py:11
  43.9 0.9 copy.33
  45.0 10.4 %fusion.84 = (f32[16,1024]{1,0:T(8,128)}, f32[16,1024,256]{1,2,0:T(8,128)}) fusion(bf16[1024,16,48]{0,2,1:T(8,128)(2,1)} %bitcast.72, bf16[256,16,48]{0,2,1:T(8,128)(2,1)S(1)} %bitcast.70), kind=kOutput, calls=%fused_computation.104 | convolution fusion | flops 415236352 | bytes 18808832 | tf_op jit(solution)/shard_map/sub | solution.py:62
  55.4 7.3 %fusion.47 = bf16[16,48,1024]{2,1,0:T(8,128)(2,1)S(1)} fusion(bf16[256,16,48]{0,2,1:T(8,128)(2,1)S(1)} %bitcast.69, f32[16,1024,256]{1,2,0:T(8,128)} %get-tuple-element.10, f32[16,1024]{1,0:T(8,128)} %get-tuple-element.9), kind=kOutput, calls=%fused_computation.55 | convolution fusion | flops 411828224 | bytes 18808832 | tf_op jit(solution)/shard_map/htk,khd->thd/dot_general | solution.py:64
  62.8 1.6 %convert_reduce_fusion.1 = (f32[1024]{0:T(1024)S(1)}, bf16[1024,768]{1,0:T(8,128)(2,1)S(1)}) fusion(bf16[1024,768]{0,1:T(8,128)(2,1)S(1)} %bitcast.74, bf16[768,768]{1,0:T(8,128)(2,1)S(1)} %copy-done, bf16[1024,768]{1,0:T(8,128)(2,1)S(1)} %copy-done.2), kind=kOutput, calls=%fused_computation.29 | convolution fusion | flops 1211890688 | bytes 5902336 | tf_op jit(solution)/shard_map/dot_general | solution.py:129
  65.5 15.5 %convert_reduce_fusion = (f32[1024]{0:T(1024)S(1)}, bf16[1024,768]{1,0:T(8,128)(2,1)S(1)}) fusion(bf16[3072,768]{1,0:T(8,128)(2,1)} %param.24, bf16[768,3072]{1,0:T(8,128)(2,1)} %param.23, bf16[1024,768]{1,0:T(8,128)(2,1)} %copy-done.8, f32[768]{0:T(1024)S(1)} %copy-done.15, f32[1024]{0:T(1024)S(1)} %add_rsqrt_fusion.1, f32[1024]{0:T(1024)S(1)} %broadcast_multiply_fusion.1), kind=kOutput, calls=%fused_computation.26 | convolution fusion | flops 9699851264 | bytes 12598272 | tf_op jit(solution)/shard_map/dot_general | solution.py:135
  82.2 1.1 copy-done.4
  84.9 23.6 %all_gather.2 = bf16[2,256,768]{2,1,0:T(8,128)(2,1)S(1)} all-gather(bf16[2,16,768]{2,1,0:T(8,128)(2,1)S(1)} %pad_maximum_fusion), channel_id=1, replica_groups=mesh['slides'=2,'seq'=16,'mp'=1] {'seq'}, dimensions={1}, use_global_device_ids=true | all-gather | bytes 835584 | tf_op jit(solution)/shard_map/all_gather | solution.py:85
  108.7 4.3 %convolution_convert_fusion = bf16[1024,768]{0,1:T(8,128)(2,1)} fusion(bf16[1024,768]{1,0:T(8,128)(2,1)} %copy-done.4, bf16[768,768]{1,0:T(8,128)(2,1)} %param.26), kind=kOutput, calls=%fused_computation.56 | convolution fusion | flops 1208745984 | bytes 4325376 | tf_op jit(solution)/shard_map/dot_general | solution.py:138
  113.2 9.7 %fusion.87 = (f32[16,1024]{1,0:T(8,128)S(1)}, f32[16,1024,256]{1,2,0:T(8,128)}) fusion(bf16[1024,16,48]{0,2,1:T(8,128)(2,1)} %bitcast.73, bf16[256,16,48]{0,2,1:T(8,128)(2,1)S(1)} %bitcast.71), kind=kOutput, calls=%fused_computation.105 | convolution fusion | flops 415236352 | bytes 18808832 | tf_op jit(solution)/shard_map/sub | solution.py:62
  122.9 7.4 %fusion.46 = bf16[16,48,1024]{2,1,0:T(8,128)(2,1)S(1)} fusion(bf16[256,16,48]{0,2,1:T(8,128)(2,1)S(1)} %bitcast.68, f32[16,1024,256]{1,2,0:T(8,128)} %get-tuple-element.16, f32[16,1024]{1,0:T(8,128)S(1)} %get-tuple-element.15), kind=kOutput, calls=%fused_computation.54 | convolution fusion | flops 411828224 | bytes 18808832 | tf_op jit(solution)/shard_map/htk,khd->thd/dot_general | solution.py:64
  130.4 2.6 %fusion.39 = bf16[1024,768]{1,0:T(8,128)(2,1)} fusion(bf16[1024,768]{1,0:T(8,128)(2,1)S(1)} %get-tuple-element.14, bf16[1024,768]{0,1:T(8,128)(2,1)S(1)} %bitcast.75, bf16[768,768]{1,0:T(8,128)(2,1)S(1)} %copy-done.14), kind=kOutput, calls=%fused_computation.50 | convolution fusion | flops 1210318848 | bytes 5898240 | tf_op jit(solution)/shard_map/dot_general | solution.py:145
  (69 shorter events, 8.9 us)
Async XLA Ops:
  0.0 62.7 %copy-start = (bf16[768,768]{1,0:T(8,128)(2,1)S(1)}, bf16[768,768]{1,0:T(8,128)(2,1)}, u32[]{:S(2)}) copy-start(bf16[768,768]{1,0:T(8,128)(2,1)} %param.21) | copy-start | bytes 3538948
  0.0 2.5 %copy-start.2 = (bf16[1024,768]{1,0:T(8,128)(2,1)S(1)}, bf16[1024,768]{1,0:T(8,128)(2,1)}, u32[]{:S(2)}) copy-start(bf16[1024,768]{1,0:T(8,128)(2,1)} %param.16) | copy-start | bytes 4718596
  0.0 3.4 %copy-start.10 = (f32[768]{0:T(1024)S(1)}, f32[768]{0:T(1024)}, u32[]{:S(2)}) copy-start(f32[768]{0:T(1024)} %param.17) | copy-start | bytes 9220
  2.5 2.6 %copy-start.12 = (s32[16]{0:T(128)S(1)}, s32[16]{0:T(128)}, u32[]{:S(2)}) copy-start(s32[16]{0:T(128)} %param.30) | copy-start | bytes 196
  2.8 2.7 %copy-start.7 = (bf16[768,768]{0,1:T(8,128)(2,1)S(1)}, bf16[768,768]{0,1:T(8,128)(2,1)}, u32[]{:S(2)}) copy-start(bf16[768,768]{0,1:T(8,128)(2,1)} %copy.27) | copy-start | bytes 3538948
  4.0 1.1 copy-start.3
  10.3 1.4 %collective-permute-start = (bf16[2,16,768]{2,1,0:T(8,128)(2,1)S(1)}, bf16[2,16,768]{2,1,0:T(8,128)(2,1)S(1)}, u32[]{:S(2)}, u32[]{:S(2)}) collective-permute-start(bf16[2,16,768]{2,1,0:T(8,128)(2,1)S(1)} %constant_dynamic-update-slice_fusion), channel_id=1, source_target_pairs={{0,1},{1,0},{2,3},{3,2},{4,5},{5,4},{6,7},{7,6},{8,9},{9,8},{10,11... | collective-permute-start | bytes 147464 | tf_op jit(solution)/shard_map/ppermute | solution.py:11
  11.8 6.0 %collective-permute-start.1 = (bf16[2,32,768]{2,1,0:T(8,128)(2,1)S(1)}, bf16[2,32,768]{2,1,0:T(8,128)(2,1)S(1)}, u32[]{:S(2)}, u32[]{:S(2)}) collective-permute-start(bf16[2,32,768]{2,1,0:T(8,128)(2,1)S(1)} %maximum_select_fusion.3), channel_id=1, source_target_pairs={{0,2},{1,3},{2,0},{3,1},{4,6},{5,7},{6,4},{7,5},{8,10},{9,11},{10,... | collective-permute-start | bytes 294920 | tf_op jit(solution)/shard_map/ppermute | solution.py:11
  17.9 6.5 %collective-permute-start.2 = (bf16[2,64,768]{2,1,0:T(8,128)(2,1)S(1)}, bf16[2,64,768]{2,1,0:T(8,128)(2,1)S(1)}, u32[]{:S(2)}, u32[]{:S(2)}) collective-permute-start(bf16[2,64,768]{2,1,0:T(8,128)(2,1)S(1)} %maximum_select_fusion.2), channel_id=1, source_target_pairs={{0,4},{1,5},{2,6},{3,7},{4,0},{5,1},{6,2},{7,3},{8,12},{9,13},{10,... | collective-permute-start | bytes 589832 | tf_op jit(solution)/shard_map/ppermute | solution.py:11
  24.4 19.1 %collective-permute-start.3 = (bf16[2,128,768]{2,1,0:T(8,128)(2,1)S(1)}, bf16[2,128,768]{2,1,0:T(8,128)(2,1)S(1)}, u32[]{:S(2)}, u32[]{:S(2)}) collective-permute-start(bf16[2,128,768]{2,1,0:T(8,128)(2,1)S(1)} %maximum_select_fusion.1), channel_id=1, source_target_pairs={{0,8},{1,9},{2,10},{3,11},{4,12},{5,13},{6,14},{7,15},{8,0},{9,1},... | collective-permute-start | bytes 1179656 | tf_op jit(solution)/shard_map/ppermute | solution.py:11
  45.0 10.4 %copy-start.9 = (bf16[1,256,768]{1,2,0:T(8,128)(2,1)S(1)}, bf16[1,256,768]{1,2,0:T(8,128)(2,1)}, u32[]{:S(2)}) copy-start(bf16[1,256,768]{1,2,0:T(8,128)(2,1)} %copy.33) | copy-start | bytes 1179652
  62.7 2.7 %copy-start.15 = (f32[768]{0:T(1024)S(1)}, f32[768]{0:T(1024)}, u32[]{:S(2)}) copy-start(f32[768]{0:T(1024)} %param.22) | copy-start | bytes 9220
  64.3 1.1 copy-start.8
  65.5 16.1 %copy-start.11 = (f32[768]{0:T(1024)S(1)}, f32[768]{0:T(1024)}, u32[]{:S(2)}) copy-start(f32[768]{0:T(1024)} %param.25) | copy-start | bytes 9220
  81.0 2.4 %copy-start.13 = (s32[16]{0:T(128)S(1)}, s32[16]{0:T(128)}, u32[]{:S(2)}) copy-start(s32[16]{0:T(128)} %param.31) | copy-start | bytes 196
  81.0 2.7 %copy-start.6 = (bf16[768,768]{0,1:T(8,128)(2,1)S(1)}, bf16[768,768]{0,1:T(8,128)(2,1)}, u32[]{:S(2)}) copy-start(bf16[768,768]{0,1:T(8,128)(2,1)} %copy.39) | copy-start | bytes 3538948
  81.6 2.7 %copy-start.5 = (bf16[768,768]{0,1:T(8,128)(2,1)S(1)}, bf16[768,768]{0,1:T(8,128)(2,1)}, u32[]{:S(2)}) copy-start(bf16[768,768]{0,1:T(8,128)(2,1)} %copy.36) | copy-start | bytes 3538948
  82.2 1.1 copy-start.4
  122.9 7.5 %copy-start.14 = (bf16[768,768]{1,0:T(8,128)(2,1)S(1)}, bf16[768,768]{1,0:T(8,128)(2,1)}, u32[]{:S(2)}) copy-start(bf16[768,768]{1,0:T(8,128)(2,1)} %param.29) | copy-start | bytes 3538948
  130.3 2.6 %copy-start.1 = (bf16[768,768]{1,0:T(8,128)(2,1)S(1)}, bf16[768,768]{1,0:T(8,128)(2,1)}, u32[]{:S(2)}) copy-start(bf16[768,768]{1,0:T(8,128)(2,1)} %param.21) | copy-start | bytes 3538948
where the time goes:
time: 133 us
  matrix products  66.8 us (50%)
  blocking collectives  23.6 us (18%)
  waiting for transfers between devices  16 us (12%)
  local copies, waits for them, and re-layouts  14.6 us (11%)
  starting transfers between devices  7.97 us (6%)
  other arithmetic  3.63 us (3%)
    all_gather x1, blocking collectives, spread_global(): keyval_two = lax.all_gather(keyval_two, 'seq', axis=1, tiled=True)  23.6 us
    sub x2, matrix products, attend_local(): weights = jnp.exp(scores - highest)  20.1 us
    ppermute x4, waiting for transfers between devices, swapped(): lax.ppermute(x, axis, [(i, i ^ 1 << apart) for i in range(lax.axis_size(a...  16 us
    dot_general x1, matrix products, body(): jnp.dot(inner, down_weight, preferred_element_type=jnp.float32)  15.5 us
    dot_general x2, matrix products, attend_local(): jnp.einsum('htk,khd->thd', weights, value_heads, preferred_element_type=j...  14.8 us
    unnamed x37, local copies, waits for them, and re-layouts  12.5 us
    ppermute x4, starting transfers between devices, swapped(): lax.ppermute(x, axis, [(i, i ^ 1 << apart) for i in range(lax.axis_size(a...  7.97 us
    dot_general x1, matrix products, body(): jnp.dot(hidden_two, query_second, preferred_element_type=jnp.float32)  4.34 us
  transfers between devices with their start and end apart: 4, of which 4 were waited for; matrix products, arithmetic and copies ran while one was open for 7% of the time, Pallas kernels for 0%

commit v1 on v0

--- a/solution.py
+++ b/solution.py
@@ -5,6 +5,29 @@
 
 KEYS = 256
 SEG_MAX = 16
+
+
+def laid_out(parts, dim):
+    parts = jnp.moveaxis(parts, 0, dim)
+    lengths = parts.shape
+    return parts.reshape(*lengths[:dim], lengths[dim] * lengths[dim + 1], *lengths[dim + 2 :])
+
+
+def collected_by_bits(x, axis):
+    size, place = (lax.axis_size(axis), lax.axis_index(axis))
+    parts, distance = (x[None], 1)
+    while distance < size:
+        partner_block = lax.ppermute(parts, axis, [(i, i ^ distance) for i in range(size)])
+        low = place & distance == 0
+        parts = jnp.concatenate(
+            [jnp.where(low, parts, partner_block), jnp.where(low, partner_block, parts)]
+        )
+        distance *= 2
+    return parts
+
+
+def gather_by_bits(x, axis, dim):
+    return laid_out(collected_by_bits(x, axis), dim)
 
 
 def swapped(x, axis, apart):
@@ -82,7 +105,7 @@
 
 
 def spread_global(keyval_two):
-    keyval_two = lax.all_gather(keyval_two, "seq", axis=1, tiled=True)
+    keyval_two = gather_by_bits(keyval_two, "seq", 1)
     return keyval_two
 
 

time: 133 us -> 144 us (1.083)
  blocking collectives: 23.6 us -> 0 us
  waiting for transfers between devices: 16 us -> 39.1 us
  local copies, waits for them, and re-layouts: 14.6 us -> 18.6 us
  starting transfers between devices: 7.97 us -> 11.8 us
  other arithmetic: 3.63 us -> 6.86 us
    all_gather x1 -> x0, blocking collectives: 23.6 us -> none  [spread_global(): keyval_two = lax.all_gather(keyval_two, 'seq', axis=1, tiled=True)]
    ppermute x0 -> x4, waiting for transfers between devices: none -> 23.1 us  [collected_by_bits(): lax.ppermute(parts, axis, [(i, i ^ distance) for i in range(size)])]
    another operation x0 -> x2, local copies, waits for them, and re-layouts: none -> 4.39 us  [the longest x1 2.2 us: attend_local(): key_heads = keyval[0].reshape(-1, head_count, head_size)]
    ppermute x0 -> x4, starting transfers between devices: none -> 3.81 us  [collected_by_bits(): lax.ppermute(parts, axis, [(i, i ^ distance) for i in range(size)])]
    reduce_sum x1, other arithmetic: 0.27 us -> 1.83 us  [norm_rows(): center = values - jnp.mean(values, axis=-1, keepdims=True)]
  transfers between devices with their start and end apart: 4 -> 8, of which waited for: 4 -> 8; matrix products, arithmetic and copies ran while one was open for 7% -> 9% of each run, Pallas kernels for 0% -> 0%
where the time goes in v1:
time: 144 us
  matrix products  67.1 us (47%)
  waiting for transfers between devices  39.1 us (27%)
  local copies, waits for them, and re-layouts  18.6 us (13%)
  starting transfers between devices  11.8 us (8%)
  other arithmetic  6.86 us (5%)
    ppermute x4, waiting for transfers between devices, collected_by_bits(): lax.ppermute(parts, axis, [(i, i ^ distance) for i in range(size)])  23.1 us
    sub x2, matrix products, attend_local(): weights = jnp.exp(scores - highest)  20 us
    ppermute x4, waiting for transfers between devices, swapped(): lax.ppermute(x, axis, [(i, i ^ 1 << apart) for i in range(lax.axis_size(a...  16 us
    dot_general x1, matrix products, body(): jnp.dot(inner, down_weight, preferred_element_type=jnp.float32)  15.5 us
    dot_general x2, matrix products, attend_local(): jnp.einsum('htk,khd->thd', weights, value_heads, preferred_element_type=j...  15.1 us
    unnamed x37, local copies, waits for them, and re-layouts  12.4 us
    ppermute x4, starting transfers between devices, swapped(): lax.ppermute(x, axis, [(i, i ^ 1 << apart) for i in range(lax.axis_size(a...  7.97 us
    dot_general x1, matrix products, body(): jnp.dot(hidden_two, query_second, preferred_element_type=jnp.float32)  4.35 us
  transfers between devices with their start and end apart: 8, of which 8 were waited for; matrix products, arithmetic and copies ran while one was open for 9% of the time, Pallas kernels for 0%

profile of v1, /device:TPU:0, one launch (start us, length us, event | category | flops | bytes accessed | tf_op | source)
XLA Modules:
  0.0 143.8 jit_solution(2183904460326714140)
XLA Ops:
  1.8 2.0 %fusion.34 = f32[1024]{0:T(1024)S(1)} fusion(bf16[1024,768]{1,0:T(8,128)(2,1)} %param.16, f32[1024]{0:T(1024)S(1)} %broadcast_multiply_fusion.2), kind=kLoop, calls=%fused_computation.45 | loop fusion | flops 3144704 | bytes 1581056 | tf_op jit(solution)/shard_map/reduce_sum | solution.py:39
  3.9 2.4 %copy.27 = bf16[768,768]{0,1:T(8,128)(2,1)} copy(bf16[768,768]{1,0:T(8,128)(2,1)} %param.19) | data formatting | bytes 2359296 | tf_op args[3]
  9.0 2.4 %copy.30 = bf16[768,768]{0,1:T(8,128)(2,1)} copy(bf16[768,768]{1,0:T(8,128)(2,1)} %param.20) | data formatting | bytes 2359296 | tf_op args[4]
  14.7 2.9 %collective-permute-start.1 = (bf16[2,32,768]{2,1,0:T(8,128)(2,1)S(1)}, bf16[2,32,768]{2,1,0:T(8,128)(2,1)S(1)}, u32[]{:S(2)}, u32[]{:S(2)}) collective-permute-start(bf16[2,32,768]{2,1,0:T(8,128)(2,1)S(1)} %maximum_select_fusion.3), channel_id=1, source_target_pairs={{0,2},{1,3},{2,0},{3,1},{4,6},{5,7},{6,4},{7,5},{8,10},{9,11},{10,... | collective-permute-start | bytes 294920 | tf_op jit(solution)/shard_map/ppermute | solution.py:34
  17.6 3.1 %collective-permute-done.1 = bf16[2,32,768]{2,1,0:T(8,128)(2,1)S(1)} collective-permute-done((bf16[2,32,768]{2,1,0:T(8,128)(2,1)S(1)}, bf16[2,32,768]{2,1,0:T(8,128)(2,1)S(1)}, u32[]{:S(2)}, u32[]{:S(2)}) %collective-permute-start.1) | collective-permute-done | bytes 98336 | tf_op jit(solution)/shard_map/ppermute | solution.py:34
  22.6 4.6 %collective-permute-done.2 = bf16[2,64,768]{2,1,0:T(8,128)(2,1)S(1)} collective-permute-done((bf16[2,64,768]{2,1,0:T(8,128)(2,1)S(1)}, bf16[2,64,768]{2,1,0:T(8,128)(2,1)S(1)}, u32[]{:S(2)}, u32[]{:S(2)}) %collective-permute-start.2) | collective-permute-done | bytes 196640 | tf_op jit(solution)/shard_map/ppermute | solution.py:34
  27.3 2.6 %collective-permute-start.3 = (bf16[2,128,768]{2,1,0:T(8,128)(2,1)S(1)}, bf16[2,128,768]{2,1,0:T(8,128)(2,1)S(1)}, u32[]{:S(2)}, u32[]{:S(2)}) collective-permute-start(bf16[2,128,768]{2,1,0:T(8,128)(2,1)S(1)} %maximum_select_fusion.1), channel_id=1, source_target_pairs={{0,8},{1,9},{2,10},{3,11},{4,12},{5,13},{6,14},{7,15},{8,0},{9,1},... | collective-permute-start | bytes 1179656 | tf_op jit(solution)/shard_map/ppermute | solution.py:34
  29.9 2.4 %copy.36 = bf16[768,768]{0,1:T(8,128)(2,1)} copy(bf16[768,768]{1,0:T(8,128)(2,1)} %param.27) | data formatting | bytes 2359296 | tf_op args[11]
  32.3 2.4 %copy.39 = bf16[768,768]{0,1:T(8,128)(2,1)} copy(bf16[768,768]{1,0:T(8,128)(2,1)} %param.28) | data formatting | bytes 2359296 | tf_op args[12]
  34.6 4.3 %convolution_convert_fusion.1 = bf16[1024,768]{0,1:T(8,128)(2,1)} fusion(bf16[1024,768]{1,0:T(8,128)(2,1)} %copy-done.4, bf16[768,768]{1,0:T(8,128)(2,1)} %param.18), kind=kOutput, calls=%fused_computation.57 | convolution fusion | flops 1208745984 | bytes 4325376 | tf_op jit(solution)/shard_map/dot_general | solution.py:147
  39.0 7.4 %collective-permute-done.3 = bf16[2,128,768]{2,1,0:T(8,128)(2,1)S(1)} collective-permute-done((bf16[2,128,768]{2,1,0:T(8,128)(2,1)S(1)}, bf16[2,128,768]{2,1,0:T(8,128)(2,1)S(1)}, u32[]{:S(2)}, u32[]{:S(2)}) %collective-permute-start.3) | collective-permute-done | bytes 393248 | tf_op jit(solution)/shard_map/ppermute | solution.py:34
  47.9 9.8 %fusion.92 = (f32[16,1024]{1,0:T(8,128)S(1)}, f32[16,1024,256]{1,2,0:T(8,128)}) fusion(bf16[1024,16,48]{0,2,1:T(8,128)(2,1)} %bitcast.82, bf16[256,16,48]{0,2,1:T(8,128)(2,1)} %bitcast.79), kind=kOutput, calls=%fused_computation.120 | convolution fusion | flops 415236352 | bytes 18808832 | tf_op jit(solution)/shard_map/sub | solution.py:85
  57.6 7.3 %fusion.46 = bf16[16,48,1024]{2,1,0:T(8,128)(2,1)S(1)} fusion(bf16[256,16,48]{0,2,1:T(8,128)(2,1)S(1)} %bitcast.80, f32[16,1024,256]{1,2,0:T(8,128)} %get-tuple-element.18, f32[16,1024]{1,0:T(8,128)S(1)} %get-tuple-element.17), kind=kOutput, calls=%fused_computation.54 | convolution fusion | flops 411828224 | bytes 18808832 | tf_op jit(solution)/shard_map/htk,khd->thd/dot_general | solution.py:87
  67.7 15.5 %convert_reduce_fusion = (f32[1024]{0:T(1024)S(1)}, bf16[1024,768]{1,0:T(8,128)(2,1)S(1)}) fusion(bf16[3072,768]{1,0:T(8,128)(2,1)} %param.24, bf16[768,3072]{1,0:T(8,128)(2,1)} %param.23, bf16[1024,768]{1,0:T(8,128)(2,1)} %copy-done.8, f32[768]{0:T(1024)S(1)} %copy-done.15, f32[1024]{0:T(1024)S(1)} %add_rsqrt_fusion.1, f32[1024]{0:T(1024)S(1)} %broadcast_multiply_fusion.1), kind=kOutput, calls=%fused_computation.26 | convolution fusion | flops 9699851264 | bytes 12598272 | tf_op jit(solution)/shard_map/dot_general | solution.py:158
  89.7 3.7 %collective-permute-done.5 = bf16[2,2,16,768]{3,2,1,0:T(8,128)(2,1)S(1)} collective-permute-done((bf16[2,2,16,768]{3,2,1,0:T(8,128)(2,1)S(1)}, bf16[2,2,16,768]{3,2,1,0:T(8,128)(2,1)S(1)}, u32[]{:S(2)}, u32[]{:S(2)}) %collective-permute-start.5) | collective-permute-done | bytes 98336 | tf_op jit(solution)/shard_map/ppermute | solution.py:20
  93.8 5.8 %collective-permute-done.6 = bf16[4,2,16,768]{3,2,1,0:T(8,128)(2,1)S(1)} collective-permute-done((bf16[4,2,16,768]{3,2,1,0:T(8,128)(2,1)S(1)}, bf16[4,2,16,768]{3,2,1,0:T(8,128)(2,1)S(1)}, u32[]{:S(2)}, u32[]{:S(2)}) %collective-permute-start.6) | collective-permute-done | bytes 196640 | tf_op jit(solution)/shard_map/ppermute | solution.py:20
  99.7 2.1 %collective-permute-start.7 = (bf16[8,2,16,768]{3,2,1,0:T(8,128)(2,1)S(1)}, bf16[8,2,16,768]{3,2,1,0:T(8,128)(2,1)S(1)}, u32[]{:S(2)}, u32[]{:S(2)}) collective-permute-start(bf16[8,2,16,768]{3,2,1,0:T(8,128)(2,1)S(1)} %pad_maximum_fusion), channel_id=1, source_target_pairs={{0,8},{1,9},{2,10},{3,11},{4,12},{5,13},{6,14},{7,15},{8,0},{9,1},... | collective-permute-start | bytes 1179656 | tf_op jit(solution)/shard_map/ppermute | solution.py:20
  101.8 4.3 %convolution_convert_fusion = bf16[1024,768]{0,1:T(8,128)(2,1)} fusion(bf16[1024,768]{1,0:T(8,128)(2,1)} %copy-done.3, bf16[768,768]{1,0:T(8,128)(2,1)} %param.26), kind=kOutput, calls=%fused_computation.56 | convolution fusion | flops 1208745984 | bytes 4325376 | tf_op jit(solution)/shard_map/dot_general | solution.py:161
  106.1 12.4 %collective-permute-done.7 = bf16[8,2,16,768]{3,2,1,0:T(8,128)(2,1)S(1)} collective-permute-done((bf16[8,2,16,768]{3,2,1,0:T(8,128)(2,1)S(1)}, bf16[8,2,16,768]{3,2,1,0:T(8,128)(2,1)S(1)}, u32[]{:S(2)}, u32[]{:S(2)}) %collective-permute-start.7) | collective-permute-done | bytes 393248 | tf_op jit(solution)/shard_map/ppermute | solution.py:20
  118.7 2.2 %reshape_squeeze.15 = bf16[256,16,48]{2,1,0:T(8,128)(2,1)} reshape(bf16[1,16,16,768]{3,2,0,1:T(8,128)(2,1)S(1)} %get-tuple-element.6) | data formatting | bytes 786432 | tf_op jit(solution)/shard_map/reshape;squeeze | solution.py:79
  120.9 2.2 %reshape_squeeze.14 = bf16[256,16,48]{2,1,0:T(8,128)(2,1)} reshape(bf16[1,16,16,768]{3,2,0,1:T(8,128)(2,1)S(1)} %get-tuple-element.5) | data formatting | bytes 786432 | tf_op jit(solution)/shard_map/reshape;squeeze | solution.py:80
  123.1 10.2 %fusion.95 = (f32[16,1024]{1,0:T(8,128)S(1)}, f32[16,1024,256]{1,2,0:T(8,128)}) fusion(bf16[1024,16,48]{0,2,1:T(8,128)(2,1)} %bitcast.81, bf16[256,16,48]{2,1,0:T(8,128)(2,1)} %reshape_squeeze.15), kind=kOutput, calls=%fused_computation.121 | convolution fusion | flops 415236352 | bytes 18808832 | tf_op jit(solution)/shard_map/sub | solution.py:85
  133.4 7.8 %fusion.47 = bf16[16,48,1024]{2,1,0:T(8,128)(2,1)S(1)} fusion(f32[16,1024,256]{1,2,0:T(8,128)} %get-tuple-element.24, f32[16,1024]{1,0:T(8,128)S(1)} %get-tuple-element.23, bf16[256,16,48]{2,1,0:T(8,128)(2,1)S(1)} %copy-done.9), kind=kOutput, calls=%fused_computation.55 | convolution fusion | flops 411828224 | bytes 18808832 | tf_op jit(solution)/shard_map/htk,khd->thd/dot_general | solution.py:87
  141.2 2.6 %fusion.39 = bf16[1024,768]{1,0:T(8,128)(2,1)} fusion(bf16[1024,768]{1,0:T(8,128)(2,1)S(1)} %get-tuple-element.22, bf16[1024,768]{0,1:T(8,128)(2,1)S(1)} %bitcast.84, bf16[768,768]{1,0:T(8,128)(2,1)S(1)} %copy-done.14), kind=kOutput, calls=%fused_computation.50 | convolution fusion | flops 1210318848 | bytes 5898240 | tf_op jit(solution)/shard_map/dot_general | solution.py:168
  (84 shorter events, 21.0 us)
Async XLA Ops:
  0.0 65.0 %copy-start = (bf16[768,768]{1,0:T(8,128)(2,1)S(1)}, bf16[768,768]{1,0:T(8,128)(2,1)}, u32[]{:S(2)}) copy-start(bf16[768,768]{1,0:T(8,128)(2,1)} %param.21) | copy-start | bytes 3538948
  0.0 6.3 %copy-start.2 = (bf16[1024,768]{1,0:T(8,128)(2,1)S(1)}, bf16[1024,768]{1,0:T(8,128)(2,1)}, u32[]{:S(2)}) copy-start(bf16[1024,768]{1,0:T(8,128)(2,1)} %param.16) | copy-start | bytes 4718596
  0.0 6.3 %copy-start.10 = (f32[768]{0:T(1024)S(1)}, f32[768]{0:T(1024)}, u32[]{:S(2)}) copy-start(f32[768]{0:T(1024)} %param.17) | copy-start | bytes 9220
  3.9 4.1 %copy-start.12 = (s32[16]{0:T(128)S(1)}, s32[16]{0:T(128)}, u32[]{:S(2)}) copy-start(s32[16]{0:T(128)} %param.30) | copy-start | bytes 196
  6.3 2.1 %copy-start.7 = (bf16[768,768]{0,1:T(8,128)(2,1)S(1)}, bf16[768,768]{0,1:T(8,128)(2,1)}, u32[]{:S(2)}) copy-start(bf16[768,768]{0,1:T(8,128)(2,1)} %copy.27) | copy-start | bytes 3538948
  6.8 1.1 copy-start.4
  13.2 1.4 %collective-permute-start = (bf16[2,16,768]{2,1,0:T(8,128)(2,1)S(1)}, bf16[2,16,768]{2,1,0:T(8,128)(2,1)S(1)}, u32[]{:S(2)}, u32[]{:S(2)}) collective-permute-start(bf16[2,16,768]{2,1,0:T(8,128)(2,1)S(1)} %constant_dynamic-update-slice_fusion), channel_id=1, source_target_pairs={{0,1},{1,0},{2,3},{3,2},{4,5},{5,4},{6,7},{7,6},{8,9},{9,8},{10,11... | collective-permute-start | bytes 147464 | tf_op jit(solution)/shard_map/ppermute | solution.py:34
  14.7 6.0 %collective-permute-start.1 = (bf16[2,32,768]{2,1,0:T(8,128)(2,1)S(1)}, bf16[2,32,768]{2,1,0:T(8,128)(2,1)S(1)}, u32[]{:S(2)}, u32[]{:S(2)}) collective-permute-start(bf16[2,32,768]{2,1,0:T(8,128)(2,1)S(1)} %maximum_select_fusion.3), channel_id=1, source_target_pairs={{0,2},{1,3},{2,0},{3,1},{4,6},{5,7},{6,4},{7,5},{8,10},{9,11},{10,... | collective-permute-start | bytes 294920 | tf_op jit(solution)/shard_map/ppermute | solution.py:34
  20.7 6.5 %collective-permute-start.2 = (bf16[2,64,768]{2,1,0:T(8,128)(2,1)S(1)}, bf16[2,64,768]{2,1,0:T(8,128)(2,1)S(1)}, u32[]{:S(2)}, u32[]{:S(2)}) collective-permute-start(bf16[2,64,768]{2,1,0:T(8,128)(2,1)S(1)} %maximum_select_fusion.2), channel_id=1, source_target_pairs={{0,4},{1,5},{2,6},{3,7},{4,0},{5,1},{6,2},{7,3},{8,12},{9,13},{10,... | collective-permute-start | bytes 589832 | tf_op jit(solution)/shard_map/ppermute | solution.py:34
  27.3 19.1 %collective-permute-start.3 = (bf16[2,128,768]{2,1,0:T(8,128)(2,1)S(1)}, bf16[2,128,768]{2,1,0:T(8,128)(2,1)S(1)}, u32[]{:S(2)}, u32[]{:S(2)}) collective-permute-start(bf16[2,128,768]{2,1,0:T(8,128)(2,1)S(1)} %maximum_select_fusion.1), channel_id=1, source_target_pairs={{0,8},{1,9},{2,10},{3,11},{4,12},{5,13},{6,14},{7,15},{8,0},{9,1},... | collective-permute-start | bytes 1179656 | tf_op jit(solution)/shard_map/ppermute | solution.py:34
  65.0 2.7 %copy-start.15 = (f32[768]{0:T(1024)S(1)}, f32[768]{0:T(1024)}, u32[]{:S(2)}) copy-start(f32[768]{0:T(1024)} %param.22) | copy-start | bytes 9220
  66.6 1.1 copy-start.8
  67.7 16.1 %copy-start.11 = (f32[768]{0:T(1024)S(1)}, f32[768]{0:T(1024)}, u32[]{:S(2)}) copy-start(f32[768]{0:T(1024)} %param.25) | copy-start | bytes 9220
  83.2 2.4 %copy-start.13 = (s32[16]{0:T(128)S(1)}, s32[16]{0:T(128)}, u32[]{:S(2)}) copy-start(s32[16]{0:T(128)} %param.31) | copy-start | bytes 196
  83.2 2.7 %copy-start.6 = (bf16[768,768]{0,1:T(8,128)(2,1)S(1)}, bf16[768,768]{0,1:T(8,128)(2,1)}, u32[]{:S(2)}) copy-start(bf16[768,768]{0,1:T(8,128)(2,1)} %copy.36) | copy-start | bytes 3538948
  83.9 2.7 %copy-start.5 = (bf16[768,768]{0,1:T(8,128)(2,1)S(1)}, bf16[768,768]{0,1:T(8,128)(2,1)}, u32[]{:S(2)}) copy-start(bf16[768,768]{0,1:T(8,128)(2,1)} %copy.39) | copy-start | bytes 3538948
  84.4 1.1 copy-start.3
  87.1 1.3 collective-permute-start.4
  88.4 4.9 %collective-permute-start.5 = (bf16[2,2,16,768]{3,2,1,0:T(8,128)(2,1)S(1)}, bf16[2,2,16,768]{3,2,1,0:T(8,128)(2,1)S(1)}, u32[]{:S(2)}, u32[]{:S(2)}) collective-permute-start(bf16[2,2,16,768]{3,2,1,0:T(8,128)(2,1)S(1)} %pad_maximum_fusion.2), channel_id=1, source_target_pairs={{0,2},{1,3},{2,0},{3,1},{4,6},{5,7},{6,4},{7,5},{8,10},{9,11},{10,... | collective-permute-start | bytes 294920 | tf_op jit(solution)/shard_map/ppermute | solution.py:20
  93.4 6.2 %collective-permute-start.6 = (bf16[4,2,16,768]{3,2,1,0:T(8,128)(2,1)S(1)}, bf16[4,2,16,768]{3,2,1,0:T(8,128)(2,1)S(1)}, u32[]{:S(2)}, u32[]{:S(2)}) collective-permute-start(bf16[4,2,16,768]{3,2,1,0:T(8,128)(2,1)S(1)} %pad_maximum_fusion.1), channel_id=1, source_target_pairs={{0,4},{1,5},{2,6},{3,7},{4,0},{5,1},{6,2},{7,3},{8,12},{9,13},{10,... | collective-permute-start | bytes 589832 | tf_op jit(solution)/shard_map/ppermute | solution.py:20
  99.7 18.9 %collective-permute-start.7 = (bf16[8,2,16,768]{3,2,1,0:T(8,128)(2,1)S(1)}, bf16[8,2,16,768]{3,2,1,0:T(8,128)(2,1)S(1)}, u32[]{:S(2)}, u32[]{:S(2)}) collective-permute-start(bf16[8,2,16,768]{3,2,1,0:T(8,128)(2,1)S(1)} %pad_maximum_fusion), channel_id=1, source_target_pairs={{0,8},{1,9},{2,10},{3,11},{4,12},{5,13},{6,14},{7,15},{8,0},{9,1},... | collective-permute-start | bytes 1179656 | tf_op jit(solution)/shard_map/ppermute | solution.py:20
  123.1 10.2 %copy-start.9 = (bf16[256,16,48]{2,1,0:T(8,128)(2,1)S(1)}, bf16[256,16,48]{2,1,0:T(8,128)(2,1)}, u32[]{:S(2)}) copy-start(bf16[256,16,48]{2,1,0:T(8,128)(2,1)} %reshape_squeeze.14) | copy-start | bytes 1179652
  133.4 7.8 %copy-start.14 = (bf16[768,768]{1,0:T(8,128)(2,1)S(1)}, bf16[768,768]{1,0:T(8,128)(2,1)}, u32[]{:S(2)}) copy-start(bf16[768,768]{1,0:T(8,128)(2,1)} %param.29) | copy-start | bytes 3538948
  141.1 2.6 %copy-start.1 = (bf16[768,768]{1,0:T(8,128)(2,1)S(1)}, bf16[768,768]{1,0:T(8,128)(2,1)}, u32[]{:S(2)}) copy-start(bf16[768,768]{1,0:T(8,128)(2,1)} %param.21) | copy-start | bytes 3538948
